TPU v7x, 1024 devices: a whole 8x8x8 slice. The times are simulated.
1024 devices in a mesh: hi: 32 (over z_hi, y), lo: 32 (over x, z_lo, core).
Axes of the slice: x: 8, y: 8, z: 8 (z_hi: 4, z_lo: 2; z = z_hi * 2 + z_lo), core: 2. Of those that a mesh axis runs over, the one named last changes fastest.
Arguments:
- state: bfloat16 [2, 268435456], P(None, ('hi', 'lo')), may hold values from -6 to 6
- gates: bfloat16 [4, 3, 2, 64, 64], replicated, may hold values from -0.5 to 0.5
- regroup: int32 [32], replicated, may hold values from 0 to 31, each once
Outputs:
- final_state: bfloat16 [2, 268435456], P(None, ('hi', 'lo'))
Inputs may be any that keep to these rules, and one draw needn't show every extreme that they name: `regroup`: each value of 0 to 31 appears once.
All inputs are finite; a program needn't handle non-finite values.
Results may differ from a plain program's by a relative error of at most 0.02.
Values may be sent and summed in bfloat16 or wider, within the bound.
A program may use at most 32 MiB of HBM per device.

v0:
```python
import functools

import jax
import jax.numpy as jnp
from jax import lax
from jax.experimental import pallas as pl
from jax.experimental.pallas import tpu as pltpu
from jax.sharding import PartitionSpec as P

BF = jnp.bfloat16
F32 = jnp.float32
MESH = pl.DeviceIdType.MESH
CH = 4


def mm(a, b):
    return lax.dot_general(a, b, (((1,), (0,)), ((), ())), preferred_element_type=F32)


def mm_t(a, b):
    return lax.dot_general(a, b, (((1,), (1,)), ((), ())), preferred_element_type=F32)


def real_form(g_ref, layer, j):
    re = g_ref[layer, j, 0]
    im = g_ref[layer, j, 1]
    upper = jnp.concatenate([re, -im], axis=1)
    lower = jnp.concatenate([im, re], axis=1)
    return jnp.concatenate([upper, lower], axis=0)


def after(second, first):
    return mm(second, first).astype(BF)


def iotas(rows, cols):
    return (
        lax.broadcasted_iota(jnp.int32, (rows, cols), 0),
        lax.broadcasted_iota(jnp.int32, (rows, cols), 1),
    )


def middle_form(whole):
    i, j = iotas(128, 128)
    pick = jnp.where(j == (i // 32 % 2) * 64 + (i % 32) * 2 + i // 64, 1.0, 0.0).astype(BF)
    sorted_rows = mm(pick, whole).astype(BF)
    both = mm_t(sorted_rows, pick)
    upper = both[:64]
    lower = pltpu.roll(both[64:], 64, 1)
    return jnp.concatenate([upper, lower], axis=0).astype(BF)


def lane_form(whole):
    i, j = iotas(256, 128)
    spread = jnp.where(j == (i // 128) * 64 + i % 64, 1.0, 0.0).astype(BF)
    tall = mm(spread, whole).astype(BF)
    wide = mm_t(tall, spread)
    i, j = iotas(256, 256)
    return jnp.where(i // 64 % 2 == j // 64 % 2, wide, 0.0).astype(BF)


def middle_operand(re, im):
    return jnp.concatenate(
        [re.astype(BF), im.astype(BF), pltpu.roll(re, 64, 1).astype(BF), pltpu.roll(im, 64, 1).astype(BF)],
        axis=0,
    )


def middle_gate(weights, pairs):
    operand = jnp.concatenate([middle_operand(re, im) for re, im in pairs], axis=1)
    made = mm(weights, operand)
    low = lax.broadcasted_iota(jnp.int32, (32, 128), 1) < 64
    out = []
    for n in range(len(pairs)):
        part = made[:, 128 * n : 128 * (n + 1)]
        out.append(
            (
                jnp.where(low, part[0:32], part[64:96]).astype(BF),
                jnp.where(low, part[32:64], part[96:128]).astype(BF),
            )
        )
    return out


def kernel(n_lo, x_ref, g_ref, rg_ref, o_ref, *scratch):
    s1 = scratch[0:4]
    y1 = scratch[4:8]
    z1 = scratch[8:12]
    r1 = scratch[12:16]
    s2 = scratch[16:20]
    y2 = scratch[20:24]
    fa, fb, wc1, wb1, wb2, wa = scratch[24:30]
    ysend, yrecv, lsend, lrecv, psend, precv, own1, own2 = scratch[30:38]
    hi = lax.axis_index("hi")
    lo = lax.axis_index("lo")
    b0, b1, b2, b3 = hi % 2, hi // 2 % 2, hi // 4 % 2, hi // 8 % 2

    def near(d):
        return hi + (1 - 2 * b0) * (d % 2) + 2 * (1 - 2 * b1) * (d // 2)

    def far(d):
        return hi + 4 * (1 - 2 * b2) * (d % 2) + 8 * (1 - 2 * b3) * (d // 2)

    barrier = pltpu.get_barrier_semaphore()
    for d in range(1, 4):
        pl.semaphore_signal(barrier, inc=1, device_id={"hi": near(d), "lo": lo}, device_id_type=MESH)
        pl.semaphore_signal(barrier, inc=1, device_id={"hi": far(d), "lo": lo}, device_id_type=MESH)

    @pl.loop(1, n_lo)
    def _(j):
        pl.semaphore_signal(
            barrier, inc=1, device_id={"hi": hi, "lo": (lo + j) % n_lo}, device_id_type=MESH
        )

    c0 = after(real_form(g_ref, 1, 2), real_form(g_ref, 0, 2))

    @pl.loop(0, 16)
    def _(i):
        made = mm(c0, x_ref[:, pl.ds(pl.multiple_of(i * 256, 256), 256)])
        fa[pl.ds(pl.multiple_of(i * 256, 256), 128), :] = made[:, :128]
        fa[pl.ds(pl.multiple_of(i * 256 + 128, 128), 128), :] = made[:, 128:]

    def from_fa(c):
        return fa[pl.ds(c, 32, stride=128), :], fa[pl.ds(64 + c, 32, stride=128), :]

    wb0 = middle_form(real_form(g_ref, 0, 1))
    pl.semaphore_wait(barrier, 6 + n_lo - 1)

    def near_copy(ch, d):
        a = b0 + (1 - 2 * b0) * (d % 2)
        b = b1 + (1 - 2 * b1) * (d // 2)
        return pltpu.make_async_remote_copy(
            src_ref=s1[ch].at[b, a],
            dst_ref=y1[ch].at[b1, b0],
            send_sem=ysend.at[ch, d],
            recv_sem=yrecv.at[ch, d],
            device_id={"hi": near(d), "lo": lo},
            device_id_type=MESH,
        )

    def lo_copy(ch, j):
        to = (lo + j) % n_lo
        return pltpu.make_async_remote_copy(
            src_ref=z1[ch].at[to],
            dst_ref=r1[ch].at[lo],
            send_sem=lsend.at[ch, j],
            recv_sem=lrecv.at[ch, j],
            device_id={"hi": hi, "lo": to},
            device_id_type=MESH,
        )

    def far_copy(ch, d):
        a = b2 + (1 - 2 * b2) * (d % 2)
        b = b3 + (1 - 2 * b3) * (d // 2)
        return pltpu.make_async_remote_copy(
            src_ref=s2[ch].at[b, a],
            dst_ref=y2[ch].at[b3, b2],
            send_sem=psend.at[ch, d],
            recv_sem=precv.at[ch, d],
            device_id={"hi": far(d), "lo": lo},
            device_id_type=MESH,
        )

    def own_near(ch):
        return pltpu.make_async_copy(s1[ch].at[b1, b0], y1[ch].at[b1, b0], own1.at[ch])

    def own_far(ch):
        return pltpu.make_async_copy(s2[ch].at[b3, b2], y2[ch].at[b3, b2], own2.at[ch])

    for q12 in range(2):

        @pl.loop(0, 16)
        def _(u):
            c = u * 2 + q12
            done = middle_gate(wb0, [from_fa(c), from_fa(c + 32)])
            for b in range(2):
                for part in range(2):
                    for a in range(2):
                        s1[q12 * 2 + part][b, a, u] = done[b][part][16 * a : 16 * (a + 1)]

        for part in range(2):
            for d in (3, 2, 1):
                near_copy(q12 * 2 + part, d).start()
            own_near(q12 * 2 + part).start()

    wc1[...] = after(real_form(g_ref, 3, 2), real_form(g_ref, 2, 2))
    wb1[...] = middle_form(after(real_form(g_ref, 2, 1), real_form(g_ref, 1, 1)))
    wb2[...] = middle_form(real_form(g_ref, 3, 1))
    lane = after(real_form(g_ref, 1, 0), real_form(g_ref, 0, 0))
    lane2 = after(real_form(g_ref, 3, 0), real_form(g_ref, 2, 0))
    wa[...] = lane_form(after(lane2, lane))

    for ch in range(CH):
        for d in range(1, 4):
            near_copy(ch, d).wait_recv()
        own_near(ch).wait()

        @pl.loop(0, n_lo)
        def _(to):
            t = rg_ref[to]
            z1[ch][to, 0] = y1[ch][t // 16, 0, t % 16]
            z1[ch][to, 1] = y1[ch][t // 16, 1, t % 16]

        @pl.loop(1, n_lo)
        def _(j):
            lo_copy(ch, j).start()

    def spread_out(ch, ref, at, t):
        q12, part = ch // 2, ch % 2
        row = (part * 64 + t * 2 + q12) * 32
        for a in range(2):
            fb[pl.ds(pl.multiple_of(row + 16 * a, 16), 16), :] = ref[at, a].astype(F32)

    for ch in range(CH):

        @pl.loop(1, n_lo)
        def _(j):
            lo_copy(ch, j).wait_recv()

        spread_out(ch, z1[ch], lo, lo)

        @pl.loop(1, n_lo)
        def _(j):
            t = (lo + j) % n_lo
            spread_out(ch, r1[ch], t, t)

    @pl.loop(0, 16)
    def _(i):
        r = i * 2
        operand = jnp.concatenate(
            [
                fb[pl.ds(r, 128, stride=32), :].astype(BF),
                fb[pl.ds(r + 1, 128, stride=32), :].astype(BF),
            ],
            axis=1,
        )
        made = mm(wc1[...], operand)
        fa[pl.ds(pl.multiple_of(i * 256, 256), 128), :] = made[:, :128]
        fa[pl.ds(pl.multiple_of(i * 256 + 128, 128), 128), :] = made[:, 128:]

    for ch in range(CH):

        @pl.loop(0, 8)
        def _(v):
            c = ch * 8 + v
            done = middle_gate(wb1[...], [from_fa(c), from_fa(c + 32)])
            for b in range(2):
                for part in range(2):
                    for a in range(2):
                        s2[ch][b, a, v, part] = done[b][part][16 * a : 16 * (a + 1)]

        for d in (3, 2, 1):
            far_copy(ch, d).start()
        own_far(ch).start()

    for ch in range(CH):
        for d in range(1, 4):
            far_copy(ch, d).wait_recv()
        own_far(ch).wait()

        @pl.loop(0, 8)
        def _(v):
            pairs = []
            for b in range(2):
                pairs.append(
                    tuple(
                        jnp.concatenate(
                            [y2[ch][b, 0, v, part], y2[ch][b, 1, v, part]], axis=0
                        ).astype(F32)
                        for part in range(2)
                    )
                )
            done = middle_gate(wb2[...], pairs)
            operand = jnp.concatenate(
                [jnp.concatenate([re, im], axis=1) for re, im in done], axis=0
            )
            made = mm_t(operand, wa[...]).astype(BF)
            for b in range(2):
                row = pl.multiple_of((b * 32 + ch * 8 + v) * 32, 32)
                for part in range(2):
                    o_ref[part, pl.ds(row, 32), :] = made[
                        32 * b : 32 * (b + 1), 128 * part : 128 * (part + 1)
                    ]

    for ch in range(CH):
        for d in range(1, 4):
            near_copy(ch, d).wait_send()
            far_copy(ch, d).wait_send()

        @pl.loop(1, n_lo)
        def _(j):
            lo_copy(ch, j).wait_send()


def on_device(state, gates, regroup):
    n_lo = lax.axis_size("lo")
    vmem = pl.BlockSpec(memory_space=pltpu.VMEM)
    x = state.reshape(128, 4096)
    quarter = (2, 2, 16, 16, 128)
    by_lo = (n_lo, 2, 16, 128)
    scratch = (
        [pltpu.VMEM(quarter, BF)] * 8
        + [pltpu.VMEM(by_lo, BF)] * 8
        + [pltpu.VMEM((2, 2, 8, 2, 16, 128), BF)] * 8
        + [pltpu.VMEM((4096, 128), F32)] * 2
        + [pltpu.VMEM((128, 128), BF)] * 3
        + [pltpu.VMEM((256, 256), BF)]
        + [pltpu.SemaphoreType.DMA((CH, 4))] * 2
        + [pltpu.SemaphoreType.DMA((CH, n_lo))] * 2
        + [pltpu.SemaphoreType.DMA((CH, 4))] * 2
        + [pltpu.SemaphoreType.DMA((CH,))] * 2
    )
    out = pl.pallas_call(
        functools.partial(kernel, n_lo),
        out_shape=jax.ShapeDtypeStruct((2, 2048, 128), BF),
        in_specs=[vmem, vmem, pl.BlockSpec(memory_space=pltpu.SMEM)],
        out_specs=vmem,
        scratch_shapes=scratch,
        compiler_params=pltpu.CompilerParams(
            collective_id=0, has_side_effects=True, vmem_limit_bytes=40 * 1024 * 1024
        ),
        name="circuit",
    )(x, gates, regroup)
    return out.reshape(2, -1)


def solution(mesh):
    placed = (P(None, ("hi", "lo")), P(), P())
    return jax.shard_map(
        on_device, mesh=mesh, in_specs=placed, out_specs=P(None, ("hi", "lo")), check_vma=False
    )
```

profile of v0, /device:TPU:1, one launch (start us, length us, event | category | flops | bytes accessed | tf_op | source)
XLA Modules:
  0.0 110.2 jit_solution(13357955233839953321)
XLA Ops:
  0.0 0.0 copy-start.1
  0.0 0.0 copy-start
  0.0 2.3 %reshape.6.x_ref = bf16[128,4096]{1,0:T(8,128)(2,1)S(1)} reshape(bf16[2,262144]{1,0:T(2,128)(2,1)} %param.3) | data formatting | bytes 2097152 | tf_op jit(solution)/shard_map/reshape | solution.py:298
  2.3 0.0 copy-done.1
  2.3 0.0 copy-done
  2.3 98.4 %circuit.1 = bf16[2,2048,128]{2,1,0:T(8,128)(2,1)S(1)} custom-call(bf16[128,4096]{1,0:T(8,128)(2,1)S(1)} %reshape.6.x_ref, bf16[4,3,2,64,64]{4,3,2,1,0:T(8,128)(2,1)S(1)} %copy-done, s32[32]{0:T(128)S(1)} %copy-done.1), custom_call_target="tpu_custom_call" | custom-call | tf_op jit(solution)/shard_map/circuit/pallas_call | solution.py:313
  100.7 9.5 %copy.6 = bf16[1,2,2048,128]{3,1,2,0:T(2,128)(2,1)} copy(bf16[1,2,2048,128]{3,2,1,0:T(8,128)(2,1)S(1)} %bitcast.4) | data formatting | bytes 2097152
Async XLA Ops:
  0.0 2.3 %copy-start.1 = (s32[32]{0:T(128)S(1)}, s32[32]{0:T(128)}, u32[]{:S(2)}) copy-start(s32[32]{0:T(128)} %rg_ref.1) | copy-start | bytes 388
  0.0 2.3 %copy-start = (bf16[4,3,2,64,64]{4,3,2,1,0:T(8,128)(2,1)S(1)}, bf16[4,3,2,64,64]{4,3,2,1,0:T(8,128)(2,1)}, u32[]{:S(2)}) copy-start(bf16[4,3,2,64,64]{4,3,2,1,0:T(8,128)(2,1)} %g_ref.1) | copy-start | bytes 589828
where the time goes:
time: 110 us
  Pallas kernels  98.4 us (89%)
  local copies, waits for them, and re-layouts  11.8 us (11%)
    pallas_call x1, Pallas kernels, on_device(): pl.pallas_call(functools.partial(kernel, n_lo), out_shape=jax.ShapeDtypeS...  98.4 us
    unnamed x5, local copies, waits for them, and re-layouts  9.47 us
    reshape x1, local copies, waits for them, and re-layouts, on_device(): x = state.reshape(128, 4096)  2.3 us

commit v1 on v0

--- a/solution.py
+++ b/solution.py
@@ -11,6 +11,8 @@
 F32 = jnp.float32
 MESH = pl.DeviceIdType.MESH
 CH = 4
+PA = 129
+PB = 33
 
 
 def mm(a, b):
@@ -40,10 +42,13 @@
     )
 
 
-def middle_form(whole):
+def middle_form(whole, paired=False):
     i, j = iotas(128, 128)
     pick = jnp.where(j == (i // 32 % 2) * 64 + (i % 32) * 2 + i // 64, 1.0, 0.0).astype(BF)
-    sorted_rows = mm(pick, whole).astype(BF)
+    order = pick
+    if paired:
+        order = jnp.where(j == (i % 2) * 64 + i // 2 % 32 * 2 + i // 64, 1.0, 0.0).astype(BF)
+    sorted_rows = mm(order, whole).astype(BF)
     both = mm_t(sorted_rows, pick)
     upper = both[:64]
     lower = pltpu.roll(both[64:], 64, 1)
@@ -53,7 +58,7 @@
 def lane_form(whole):
     i, j = iotas(256, 128)
     spread = jnp.where(j == (i // 128) * 64 + i % 64, 1.0, 0.0).astype(BF)
-    tall = mm(spread, whole).astype(BF)
+    tall = mm_t(spread, whole).astype(BF)
     wide = mm_t(tall, spread)
     i, j = iotas(256, 256)
     return jnp.where(i // 64 % 2 == j // 64 % 2, wide, 0.0).astype(BF)
@@ -90,7 +95,7 @@
     s2 = scratch[16:20]
     y2 = scratch[20:24]
     fa, fb, wc1, wb1, wb2, wa = scratch[24:30]
-    ysend, yrecv, lsend, lrecv, psend, precv, own1, own2 = scratch[30:38]
+    ysend, yrecv, lsend, lrecv, psend, precv = scratch[30:36]
     hi = lax.axis_index("hi")
     lo = lax.axis_index("lo")
     b0, b1, b2, b3 = hi % 2, hi // 2 % 2, hi // 4 % 2, hi // 8 % 2
@@ -114,14 +119,14 @@
 
     c0 = after(real_form(g_ref, 1, 2), real_form(g_ref, 0, 2))
 
-    @pl.loop(0, 16)
+    @pl.loop(0, 16, unroll=4)
     def _(i):
         made = mm(c0, x_ref[:, pl.ds(pl.multiple_of(i * 256, 256), 256)])
-        fa[pl.ds(pl.multiple_of(i * 256, 256), 128), :] = made[:, :128]
-        fa[pl.ds(pl.multiple_of(i * 256 + 128, 128), 128), :] = made[:, 128:]
+        fa[pl.ds(2 * i * PA, 128), :] = made[:, :128]
+        fa[pl.ds(2 * i * PA + PA, 128), :] = made[:, 128:]
 
     def from_fa(c):
-        return fa[pl.ds(c, 32, stride=128), :], fa[pl.ds(64 + c, 32, stride=128), :]
+        return fa[pl.ds(c, 32, stride=PA), :], fa[pl.ds(64 + c, 32, stride=PA), :]
 
     wb0 = middle_form(real_form(g_ref, 0, 1))
     pl.semaphore_wait(barrier, 6 + n_lo - 1)
@@ -162,14 +167,14 @@
         )
 
     def own_near(ch):
-        return pltpu.make_async_copy(s1[ch].at[b1, b0], y1[ch].at[b1, b0], own1.at[ch])
+        y1[ch][b1, b0] = s1[ch][b1, b0]
 
     def own_far(ch):
-        return pltpu.make_async_copy(s2[ch].at[b3, b2], y2[ch].at[b3, b2], own2.at[ch])
+        y2[ch][b3, b2] = s2[ch][b3, b2]
 
     for q12 in range(2):
 
-        @pl.loop(0, 16)
+        @pl.loop(0, 16, unroll=4)
         def _(u):
             c = u * 2 + q12
             done = middle_gate(wb0, [from_fa(c), from_fa(c + 32)])
@@ -181,11 +186,11 @@
         for part in range(2):
             for d in (3, 2, 1):
                 near_copy(q12 * 2 + part, d).start()
-            own_near(q12 * 2 + part).start()
+            own_near(q12 * 2 + part)
 
     wc1[...] = after(real_form(g_ref, 3, 2), real_form(g_ref, 2, 2))
     wb1[...] = middle_form(after(real_form(g_ref, 2, 1), real_form(g_ref, 1, 1)))
-    wb2[...] = middle_form(real_form(g_ref, 3, 1))
+    wb2[...] = middle_form(real_form(g_ref, 3, 1), paired=True)
     lane = after(real_form(g_ref, 1, 0), real_form(g_ref, 0, 0))
     lane2 = after(real_form(g_ref, 3, 0), real_form(g_ref, 2, 0))
     wa[...] = lane_form(after(lane2, lane))
@@ -193,9 +198,8 @@
     for ch in range(CH):
         for d in range(1, 4):
             near_copy(ch, d).wait_recv()
-        own_near(ch).wait()
-
-        @pl.loop(0, n_lo)
+
+        @pl.loop(0, n_lo, unroll=4)
         def _(to):
             t = rg_ref[to]
             z1[ch][to, 0] = y1[ch][t // 16, 0, t % 16]
@@ -207,9 +211,9 @@
 
     def spread_out(ch, ref, at, t):
         q12, part = ch // 2, ch % 2
-        row = (part * 64 + t * 2 + q12) * 32
+        row = (part * 64 + t * 2 + q12) * PB
         for a in range(2):
-            fb[pl.ds(pl.multiple_of(row + 16 * a, 16), 16), :] = ref[at, a].astype(F32)
+            fb[pl.ds(row + 16 * a, 16), :] = ref[at, a].astype(F32)
 
     for ch in range(CH):
 
@@ -224,23 +228,23 @@
             t = (lo + j) % n_lo
             spread_out(ch, r1[ch], t, t)
 
-    @pl.loop(0, 16)
+    @pl.loop(0, 16, unroll=4)
     def _(i):
         r = i * 2
         operand = jnp.concatenate(
             [
-                fb[pl.ds(r, 128, stride=32), :].astype(BF),
-                fb[pl.ds(r + 1, 128, stride=32), :].astype(BF),
+                fb[pl.ds(r, 128, stride=PB), :].astype(BF),
+                fb[pl.ds(r + 1, 128, stride=PB), :].astype(BF),
             ],
             axis=1,
         )
         made = mm(wc1[...], operand)
-        fa[pl.ds(pl.multiple_of(i * 256, 256), 128), :] = made[:, :128]
-        fa[pl.ds(pl.multiple_of(i * 256 + 128, 128), 128), :] = made[:, 128:]
-
-    for ch in range(CH):
-
-        @pl.loop(0, 8)
+        fa[pl.ds(2 * i * PA, 128), :] = made[:, :128]
+        fa[pl.ds(2 * i * PA + PA, 128), :] = made[:, 128:]
+
+    for ch in range(CH):
+
+        @pl.loop(0, 8, unroll=4)
         def _(v):
             c = ch * 8 + v
             done = middle_gate(wb1[...], [from_fa(c), from_fa(c + 32)])
@@ -251,36 +255,37 @@
 
         for d in (3, 2, 1):
             far_copy(ch, d).start()
-        own_far(ch).start()
+        own_far(ch)
 
     for ch in range(CH):
         for d in range(1, 4):
             far_copy(ch, d).wait_recv()
-        own_far(ch).wait()
-
-        @pl.loop(0, 8)
-        def _(v):
-            pairs = []
-            for b in range(2):
-                pairs.append(
-                    tuple(
-                        jnp.concatenate(
-                            [y2[ch][b, 0, v, part], y2[ch][b, 1, v, part]], axis=0
-                        ).astype(F32)
-                        for part in range(2)
-                    )
-                )
-            done = middle_gate(wb2[...], pairs)
+
+        @pl.loop(0, 2)
+        def _(g):
+            rows = []
+            for k in range(4):
+                for b in range(2):
+                    for a in range(2):
+                        rows.append(
+                            jnp.concatenate(
+                                [y2[ch][b, a, g * 4 + k, 0], y2[ch][b, a, g * 4 + k, 1]], axis=1
+                            )
+                        )
+            made = mm(jnp.concatenate(rows, axis=0), wa[...])
             operand = jnp.concatenate(
-                [jnp.concatenate([re, im], axis=1) for re, im in done], axis=0
+                [
+                    middle_operand(made[32 * n : 32 * n + 32, :128], made[32 * n : 32 * n + 32, 128:])
+                    for n in range(8)
+                ],
+                axis=1,
             )
-            made = mm_t(operand, wa[...]).astype(BF)
-            for b in range(2):
-                row = pl.multiple_of((b * 32 + ch * 8 + v) * 32, 32)
-                for part in range(2):
-                    o_ref[part, pl.ds(row, 32), :] = made[
-                        32 * b : 32 * (b + 1), 128 * part : 128 * (part + 1)
-                    ]
+            whole = mm(wb2[...], operand)
+            low = lax.broadcasted_iota(jnp.int32, (64, 128), 1) < 64
+            for n in range(8):
+                row = pl.multiple_of((n % 2 * 32 + ch * 8 + g * 4 + n // 2) * 64, 64)
+                part = whole[:, 128 * n : 128 * (n + 1)]
+                o_ref[pl.ds(row, 64), :] = jnp.where(low, part[:64], part[64:]).astype(BF)
 
     for ch in range(CH):
         for d in range(1, 4):
@@ -302,17 +307,16 @@
         [pltpu.VMEM(quarter, BF)] * 8
         + [pltpu.VMEM(by_lo, BF)] * 8
         + [pltpu.VMEM((2, 2, 8, 2, 16, 128), BF)] * 8
-        + [pltpu.VMEM((4096, 128), F32)] * 2
+        + [pltpu.VMEM((32 * PA, 128), F32), pltpu.VMEM((128 * PB, 128), F32)]
         + [pltpu.VMEM((128, 128), BF)] * 3
         + [pltpu.VMEM((256, 256), BF)]
         + [pltpu.SemaphoreType.DMA((CH, 4))] * 2
         + [pltpu.SemaphoreType.DMA((CH, n_lo))] * 2
         + [pltpu.SemaphoreType.DMA((CH, 4))] * 2
-        + [pltpu.SemaphoreType.DMA((CH,))] * 2
     )
     out = pl.pallas_call(
         functools.partial(kernel, n_lo),
-        out_shape=jax.ShapeDtypeStruct((2, 2048, 128), BF),
+        out_shape=jax.ShapeDtypeStruct((4096, 128), BF),
         in_specs=[vmem, vmem, pl.BlockSpec(memory_space=pltpu.SMEM)],
         out_specs=vmem,
         scratch_shapes=scratch,
@@ -321,7 +325,7 @@
         ),
         name="circuit",
     )(x, gates, regroup)
-    return out.reshape(2, -1)
+    return out.reshape(2048, 2, 128).transpose(1, 0, 2).reshape(2, -1)
 
 
 def solution(mesh):

time: 110 us -> 91.8 us (0.83)
  Pallas kernels: 98.4 us -> 88.3 us
  local copies, waits for them, and re-layouts: 11.8 us -> 3.28 us
    pallas_call x1, Pallas kernels: 98.4 us -> 88.3 us  [on_device(): pl.pallas_call(functools.partial(kernel, n_lo), out_shape=jax.ShapeDtypeS...]
    unnamed x5, local copies, waits for them, and re-layouts: 9.47 us -> 0.98 us
where the time goes in v1:
time: 91.8 us; the launch traced here: 91.6 us
  Pallas kernels  88.3 us (96%)
  local copies, waits for them, and re-layouts  3.28 us (4%)
    pallas_call x1, Pallas kernels, on_device(): pl.pallas_call(functools.partial(kernel, n_lo), out_shape=jax.ShapeDtypeS...  88.3 us
    reshape x1, local copies, waits for them, and re-layouts, on_device(): x = state.reshape(128, 4096)  2.3 us

profile of v1, /device:TPU:1, one launch (start us, length us, event | category | flops | bytes accessed | tf_op | source)
XLA Modules:
  0.0 91.6 jit_solution(7392431767493490292)
XLA Ops:
  0.0 0.0 copy-start.1
  0.0 0.0 copy-start
  0.0 2.3 %reshape.9.x_ref = bf16[128,4096]{1,0:T(8,128)(2,1)S(1)} reshape(bf16[2,262144]{1,0:T(2,128)(2,1)} %param.3) | data formatting | bytes 2097152 | tf_op jit(solution)/shard_map/reshape | solution.py:303
  2.3 0.0 copy-done.1
  2.3 0.0 copy-done
  2.3 88.3 %circuit.1 = bf16[4096,128]{1,0:T(8,128)(2,1)S(1)} custom-call(bf16[128,4096]{1,0:T(8,128)(2,1)S(1)} %reshape.9.x_ref, bf16[4,3,2,64,64]{4,3,2,1,0:T(8,128)(2,1)S(1)} %copy-done, s32[32]{0:T(128)S(1)} %copy-done.1), custom_call_target="tpu_custom_call" | custom-call | tf_op jit(solution)/shard_map/circuit/pallas_call | solution.py:317
  90.6 1.0 %copy.6 = bf16[2,262144]{1,0:T(2,128)(2,1)} copy(bf16[2,262144]{1,0:T(2,128)(2,1)S(1)} %bitcast.5) | data formatting | bytes 2097152
Async XLA Ops:
  0.0 2.3 %copy-start.1 = (s32[32]{0:T(128)S(1)}, s32[32]{0:T(128)}, u32[]{:S(2)}) copy-start(s32[32]{0:T(128)} %rg_ref.1) | copy-start | bytes 388
  0.0 2.3 %copy-start = (bf16[4,3,2,64,64]{4,3,2,1,0:T(8,128)(2,1)S(1)}, bf16[4,3,2,64,64]{4,3,2,1,0:T(8,128)(2,1)}, u32[]{:S(2)}) copy-start(bf16[4,3,2,64,64]{4,3,2,1,0:T(8,128)(2,1)} %g_ref.1) | copy-start | bytes 589828

commit v2 on v1

v2 whole, which is shorter than its diff:
```python
import functools

import jax
import jax.numpy as jnp
from jax import lax
from jax.experimental import pallas as pl
from jax.experimental.pallas import tpu as pltpu
from jax.sharding import PartitionSpec as P

BF = jnp.bfloat16
F32 = jnp.float32
MESH = pl.DeviceIdType.MESH
CH = 4
SUB = 4
PA = 129
PB = 33
PC = 65


def mm(a, b):
    return lax.dot_general(a, b, (((1,), (0,)), ((), ())), preferred_element_type=F32)


def mm_t(a, b):
    return lax.dot_general(a, b, (((1,), (1,)), ((), ())), preferred_element_type=F32)


def real_form(g_ref, layer, j):
    re = g_ref[layer, j, 0]
    im = g_ref[layer, j, 1]
    upper = jnp.concatenate([re, -im], axis=1)
    lower = jnp.concatenate([im, re], axis=1)
    return jnp.concatenate([upper, lower], axis=0)


def after(second, first):
    return mm(second, first).astype(BF)


def iotas(rows, cols):
    return (
        lax.broadcasted_iota(jnp.int32, (rows, cols), 0),
        lax.broadcasted_iota(jnp.int32, (rows, cols), 1),
    )


def middle_form(whole, paired=False):
    i, j = iotas(128, 128)
    pick = jnp.where(j == (i // 32 % 2) * 64 + (i % 32) * 2 + i // 64, 1.0, 0.0).astype(BF)
    order = pick
    if paired:
        order = jnp.where(j == (i % 2) * 64 + i // 2 % 32 * 2 + i // 64, 1.0, 0.0).astype(BF)
    both = mm_t(mm(order, whole).astype(BF), pick)
    return jnp.concatenate([both[:64], pltpu.roll(both[64:], 64, 1)], axis=0).astype(BF)


def quarter_form(whole):
    i, j = iotas(128, 128)
    pick = jnp.where(j == (i // 64) * 64 + (i % 32) * 2 + i // 32 % 2, 1.0, 0.0).astype(BF)
    both = mm_t(mm(pick, whole).astype(BF), pick)
    rows = [both[:32]]
    for n in range(1, 4):
        rows.append(pltpu.roll(both[32 * n : 32 * n + 32], 128 - 32 * n, 1))
    return jnp.concatenate(rows, axis=0).astype(BF)


def half_form(whole):
    lower = pltpu.roll(whole[64:].astype(F32), 64, 1)
    return jnp.concatenate([whole[:64], lower.astype(BF)], axis=0)


def regrouped(i):
    return (i // 32 % 2) * 128 + (i // 128) * 64 + (i // 64 % 2) * 32 + i % 32


def lane_form(whole):
    i, j = iotas(256, 128)
    spread = jnp.where(j == (i // 128) * 64 + i % 64, 1.0, 0.0).astype(BF)
    wide = mm_t(mm_t(spread, whole).astype(BF), spread)
    i, j = iotas(256, 256)
    natural = jnp.where(i // 64 % 2 == j // 64 % 2, wide, 0.0).astype(BF)
    back = jnp.where(i == regrouped(j), 1.0, 0.0).astype(BF)
    return mm(back, natural).astype(BF)


def middle_operand(re, im):
    return jnp.concatenate(
        [re.astype(BF), im.astype(BF), pltpu.roll(re, 64, 1).astype(BF), pltpu.roll(im, 64, 1).astype(BF)],
        axis=0,
    )


def kernel(n_lo, x_ref, g_ref, rg_ref, o_ref, *scratch):
    s1 = scratch[0:4]
    y1 = scratch[4:8]
    z1 = scratch[8:12]
    r1 = scratch[12:16]
    s2 = scratch[16:24]
    y2 = scratch[24:32]
    m2 = scratch[32:40]
    fa, fb, wc1, wb1, wb2, wa, perm = scratch[40:47]
    ysend, yrecv, lsend, lrecv, psend, precv = scratch[47:53]
    hi = lax.axis_index("hi")
    lo = lax.axis_index("lo")
    b0, b1, b2, b3 = hi % 2, hi // 2 % 2, hi // 4 % 2, hi // 8 % 2
    y_peer = hi + 4 * (1 - 2 * b2)
    z_peer = hi + 8 * (1 - 2 * b3)

    def near(d):
        return hi + (1 - 2 * b0) * (d % 2) + 2 * (1 - 2 * b1) * (d // 2)

    barrier = pltpu.get_barrier_semaphore()
    for to in (near(1), near(2), near(3), y_peer, z_peer):
        pl.semaphore_signal(barrier, inc=1, device_id={"hi": to, "lo": lo}, device_id_type=MESH)

    @pl.loop(1, n_lo)
    def _(j):
        pl.semaphore_signal(
            barrier, inc=1, device_id={"hi": hi, "lo": (lo + j) % n_lo}, device_id_type=MESH
        )

    c0 = after(real_form(g_ref, 1, 2), real_form(g_ref, 0, 2))

    @pl.loop(0, 16, unroll=4)
    def _(i):
        made = mm(c0, x_ref[:, pl.ds(pl.multiple_of(i * 256, 256), 256)])
        fa[pl.ds(2 * i * PA, 128), :] = made[:, :128]
        fa[pl.ds(2 * i * PA + PA, 128), :] = made[:, 128:]

    wb0 = middle_form(real_form(g_ref, 0, 1))
    i, j = iotas(256, 256)
    perm[...] = jnp.where(j == regrouped(i), 1.0, 0.0).astype(BF)
    pl.semaphore_wait(barrier, 5 + n_lo - 1)

    def near_copy(ch, d):
        a = b0 + (1 - 2 * b0) * (d % 2)
        b = b1 + (1 - 2 * b1) * (d // 2)
        return pltpu.make_async_remote_copy(
            src_ref=s1[ch].at[b, a],
            dst_ref=y1[ch].at[b1, b0],
            send_sem=ysend.at[ch, d],
            recv_sem=yrecv.at[ch, d],
            device_id={"hi": near(d), "lo": lo},
            device_id_type=MESH,
        )

    def lo_copy(ch, j):
        to = (lo + j) % n_lo
        return pltpu.make_async_remote_copy(
            src_ref=z1[ch].at[to],
            dst_ref=r1[ch].at[lo],
            send_sem=lsend.at[ch, j],
            recv_sem=lrecv.at[ch, j],
            device_id={"hi": hi, "lo": to},
            device_id_type=MESH,
        )

    def far_copy(k, kind):
        src, dst, to = (
            (m2[k], y2[k].at[1 - b3, b2], y_peer),
            (s2[k].at[b3, 1 - b2], y2[k].at[b3, b2], y_peer),
            (s2[k].at[1 - b3, b2], y2[k].at[b3, b2], z_peer),
            (s2[k].at[1 - b3, 1 - b2], m2[k], z_peer),
        )[kind]
        return pltpu.make_async_remote_copy(
            src_ref=src,
            dst_ref=dst,
            send_sem=psend.at[k, kind],
            recv_sem=precv.at[k, kind],
            device_id={"hi": to, "lo": lo},
            device_id_type=MESH,
        )

    def send_near(ch):
        for d in (3, 2, 1):
            near_copy(ch, d).start()
        y1[ch][b1, b0] = s1[ch][b1, b0]

    low = lax.broadcasted_iota(jnp.int32, (32, 128), 1) < 64
    for q12 in range(2):

        @pl.loop(0, 4)
        def _(g):
            parts = []
            for k in range(4):
                for b in range(2):
                    c = b * 32 + (g * 4 + k) * 2 + q12
                    parts.append(
                        middle_operand(
                            fa[pl.ds(c, 32, stride=PA), :], fa[pl.ds(64 + c, 32, stride=PA), :]
                        )
                    )
            made = mm(wb0, jnp.concatenate(parts, axis=1))
            rows = []
            for n in range(8):
                part = made[:, 128 * n : 128 * (n + 1)]
                re = jnp.where(low, part[0:32], part[64:96]).astype(BF)
                im = jnp.where(low, part[32:64], part[96:128]).astype(BF)
                rows.append(jnp.concatenate([re, im], axis=1))
            moved = mm(jnp.concatenate(rows, axis=0), perm[...]).astype(BF)
            for n in range(8):
                for e in range(2):
                    for a in range(2):
                        s1[e * 2 + q12][n % 2, a, g * 4 + n // 2] = moved[
                            32 * n + 16 * a : 32 * n + 16 * a + 16, 128 * e : 128 * (e + 1)
                        ]

        send_near(q12)
    send_near(2)
    send_near(3)

    wc1[...] = half_form(after(real_form(g_ref, 3, 2), real_form(g_ref, 2, 2)))
    wb1[...] = quarter_form(after(real_form(g_ref, 2, 1), real_form(g_ref, 1, 1)))
    wb2[...] = middle_form(real_form(g_ref, 3, 1), paired=True)
    lane = after(real_form(g_ref, 1, 0), real_form(g_ref, 0, 0))
    lane2 = after(real_form(g_ref, 3, 0), real_form(g_ref, 2, 0))
    wa[...] = lane_form(after(lane2, lane))

    def pass_to_lo(ch):
        for d in range(1, 4):
            near_copy(ch, d).wait_recv()

        @pl.loop(0, n_lo, unroll=4)
        def _(to):
            t = rg_ref[to]
            z1[ch][to, 0] = y1[ch][t // 16, 0, t % 16]
            z1[ch][to, 1] = y1[ch][t // 16, 1, t % 16]

        @pl.loop(1, n_lo)
        def _(j):
            lo_copy(ch, j).start()

    def spread_out(ch, ref, t):
        for a in range(2):
            fb[pl.ds((t * 2 + ch % 2) * PB + 16 * a, 16), :] = ref[t, a].astype(F32)

    def take_from_lo(ch):
        spread_out(ch, z1[ch], lo)

        @pl.loop(1, n_lo)
        def _(j):
            lo_copy(ch, j).wait_recv()

        @pl.loop(1, n_lo)
        def _(j):
            spread_out(ch, r1[ch], (lo + j) % n_lo)

    def top_gate():
        left = lax.broadcasted_iota(jnp.int32, (64, 128), 1) < 64

        @pl.loop(0, 8)
        def _(g):
            parts = []
            for k in range(4):
                x = fb[pl.ds(g * 4 + k, 64, stride=PB), :]
                parts.append(
                    jnp.concatenate([x.astype(BF), pltpu.roll(x, 64, 1).astype(BF)], axis=0)
                )
            made = mm(wc1[...], jnp.concatenate(parts, axis=1))
            for k in range(4):
                part = made[:, 128 * k : 128 * (k + 1)]
                fa[pl.ds((g * 4 + k) * PC, 64), :] = jnp.where(left, part[:64], part[64:])

    quarter = lax.broadcasted_iota(jnp.int32, (32, 128), 1) // 32

    def middle_and_send(e, n_sub):
        at = e * SUB + n_sub

        @pl.loop(0, 2)
        def _(g):
            parts = []
            for k in range(4):
                for b in range(2):
                    x = fa[pl.ds(b * 32 + n_sub * 8 + g * 4 + k, 32, stride=PC), :]
                    parts.append(
                        jnp.concatenate(
                            [x.astype(BF)]
                            + [pltpu.roll(x, 128 - 32 * m, 1).astype(BF) for m in range(1, 4)],
                            axis=0,
                        )
                    )
            made = mm(wb1[...], jnp.concatenate(parts, axis=1))
            for n in range(8):
                part = made[:, 128 * n : 128 * (n + 1)]
                first = jnp.where(quarter == 0, part[0:32], part[32:64])
                second = jnp.where(quarter == 2, part[64:96], part[96:128])
                done = jnp.where(quarter < 2, first, second).astype(BF)
                for a in range(2):
                    s2[at][n % 2, a, g * 4 + n // 2] = done[16 * a : 16 * (a + 1)]

        for kind in (3, 1, 2):
            far_copy(at, kind).start()
        y2[at][b3, b2] = s2[at][b3, b2]

    def pass_on(at):
        far_copy(at, 3).wait_recv()
        far_copy(at, 0).start()

    pass_to_lo(0)
    pass_to_lo(1)
    take_from_lo(0)
    take_from_lo(1)
    top_gate()
    for n_sub in range(SUB):
        middle_and_send(0, n_sub)
    pass_to_lo(2)
    pass_on(0)
    pass_on(1)
    pass_to_lo(3)
    pass_on(2)
    pass_on(3)
    take_from_lo(2)
    take_from_lo(3)
    top_gate()
    for n_sub in range(SUB):
        middle_and_send(1, n_sub)
    for n_sub in range(SUB):
        pass_on(SUB + n_sub)

    for ch in range(SUB):
        for e in range(2):
            for kind in range(3):
                far_copy(e * SUB + ch, kind).wait_recv()

        @pl.loop(0, 2)
        def _(g):
            rows = []
            for k in range(4):
                for b in range(2):
                    for a in range(2):
                        rows.append(
                            jnp.concatenate(
                                [y2[ch][b, a, g * 4 + k], y2[SUB + ch][b, a, g * 4 + k]], axis=1
                            )
                        )
            made = mm(jnp.concatenate(rows, axis=0), wa[...])
            operand = jnp.concatenate(
                [
                    middle_operand(made[32 * n : 32 * n + 32, :128], made[32 * n : 32 * n + 32, 128:])
                    for n in range(8)
                ],
                axis=1,
            )
            whole = mm(wb2[...], operand)
            left = lax.broadcasted_iota(jnp.int32, (64, 128), 1) < 64
            for n in range(8):
                row = pl.multiple_of((n % 2 * 32 + ch * 8 + g * 4 + n // 2) * 64, 64)
                part = whole[:, 128 * n : 128 * (n + 1)]
                o_ref[pl.ds(row, 64), :] = jnp.where(left, part[:64], part[64:]).astype(BF)

    for ch in range(CH):
        for d in range(1, 4):
            near_copy(ch, d).wait_send()

        @pl.loop(1, n_lo)
        def _(j):
            lo_copy(ch, j).wait_send()

    for at in range(2 * SUB):
        for kind in range(4):
            far_copy(at, kind).wait_send()


def on_device(state, gates, regroup):
    n_lo = lax.axis_size("lo")
    vmem = pl.BlockSpec(memory_space=pltpu.VMEM)
    x = state.reshape(128, 4096)
    quarter = (2, 2, 16, 16, 128)
    by_lo = (n_lo, 2, 16, 128)
    scratch = (
        [pltpu.VMEM(quarter, BF)] * 8
        + [pltpu.VMEM(by_lo, BF)] * 8
        + [pltpu.VMEM((2, 2, 8, 16, 128), BF)] * 16
        + [pltpu.VMEM((8, 16, 128), BF)] * 8
        + [pltpu.VMEM((32 * PA, 128), F32), pltpu.VMEM((64 * PB, 128), F32)]
        + [pltpu.VMEM((128, 128), BF)] * 3
        + [pltpu.VMEM((256, 256), BF)] * 2
        + [pltpu.SemaphoreType.DMA((CH, 4))] * 2
        + [pltpu.SemaphoreType.DMA((CH, n_lo))] * 2
        + [pltpu.SemaphoreType.DMA((2 * SUB, 4))] * 2
    )
    out = pl.pallas_call(
        functools.partial(kernel, n_lo),
        out_shape=jax.ShapeDtypeStruct((4096, 128), BF),
        in_specs=[vmem, vmem, pl.BlockSpec(memory_space=pltpu.SMEM)],
        out_specs=vmem,
        scratch_shapes=scratch,
        compiler_params=pltpu.CompilerParams(
            collective_id=0, has_side_effects=True, vmem_limit_bytes=40 * 1024 * 1024
        ),
        name="circuit",
    )(x, gates, regroup)
    return out.reshape(2048, 2, 128).transpose(1, 0, 2).reshape(2, -1)


def solution(mesh):
    placed = (P(None, ("hi", "lo")), P(), P())
    return jax.shard_map(
        on_device, mesh=mesh, in_specs=placed, out_specs=P(None, ("hi", "lo")), check_vma=False
    )
```

time: 91.8 us -> 97 us (1.057)
  Pallas kernels: 88.3 us -> 93.5 us
    pallas_call x1, Pallas kernels: 88.3 us -> 93.5 us  [on_device(): pl.pallas_call(functools.partial(kernel, n_lo), out_shape=jax.ShapeDtypeS...]
where the time goes in v2:
time: 97 us; the launch traced here: 96.8 us
  Pallas kernels  93.5 us (96%)
  local copies, waits for them, and re-layouts  3.28 us (3%)
    pallas_call x1, Pallas kernels, on_device(): pl.pallas_call(functools.partial(kernel, n_lo), out_shape=jax.ShapeDtypeS...  93.5 us
    reshape x1, local copies, waits for them, and re-layouts, on_device(): x = state.reshape(128, 4096)  2.3 us

profile of v2, /device:TPU:1, one launch (start us, length us, event | category | flops | bytes accessed | tf_op | source)
XLA Modules:
  0.0 96.8 jit_solution(5325526810655578171)
XLA Ops:
  0.0 0.0 copy-start.1
  0.0 0.0 copy-start
  0.0 2.3 %reshape.9.x_ref = bf16[128,4096]{1,0:T(8,128)(2,1)S(1)} reshape(bf16[2,262144]{1,0:T(2,128)(2,1)} %param.3) | data formatting | bytes 2097152 | tf_op jit(solution)/shard_map/reshape | solution.py:367
  2.3 0.0 copy-done.1
  2.3 0.0 copy-done
  2.3 93.5 %circuit.1 = bf16[4096,128]{1,0:T(8,128)(2,1)S(1)} custom-call(bf16[128,4096]{1,0:T(8,128)(2,1)S(1)} %reshape.9.x_ref, bf16[4,3,2,64,64]{4,3,2,1,0:T(8,128)(2,1)S(1)} %copy-done, s32[32]{0:T(128)S(1)} %copy-done.1), custom_call_target="tpu_custom_call" | custom-call | tf_op jit(solution)/shard_map/circuit/pallas_call | solution.py:382
  95.8 1.0 %copy.6 = bf16[2,262144]{1,0:T(2,128)(2,1)} copy(bf16[2,262144]{1,0:T(2,128)(2,1)S(1)} %bitcast.5) | data formatting | bytes 2097152
Async XLA Ops:
  0.0 2.3 %copy-start.1 = (s32[32]{0:T(128)S(1)}, s32[32]{0:T(128)}, u32[]{:S(2)}) copy-start(s32[32]{0:T(128)} %rg_ref.1) | copy-start | bytes 388
  0.0 2.3 %copy-start = (bf16[4,3,2,64,64]{4,3,2,1,0:T(8,128)(2,1)S(1)}, bf16[4,3,2,64,64]{4,3,2,1,0:T(8,128)(2,1)}, u32[]{:S(2)}) copy-start(bf16[4,3,2,64,64]{4,3,2,1,0:T(8,128)(2,1)} %g_ref.1) | copy-start | bytes 589828

commit v3 on v2

--- a/solution.py
+++ b/solution.py
@@ -97,20 +97,20 @@
     r1 = scratch[12:16]
     s2 = scratch[16:24]
     y2 = scratch[24:32]
-    m2 = scratch[32:40]
-    fa, fb, wc1, wb1, wb2, wa, perm = scratch[40:47]
-    ysend, yrecv, lsend, lrecv, psend, precv = scratch[47:53]
+    fa, fb, wc1, wb1, wb2, wa, perm = scratch[32:39]
+    ysend, yrecv, lsend, lrecv, psend, precv = scratch[39:45]
     hi = lax.axis_index("hi")
     lo = lax.axis_index("lo")
     b0, b1, b2, b3 = hi % 2, hi // 2 % 2, hi // 4 % 2, hi // 8 % 2
-    y_peer = hi + 4 * (1 - 2 * b2)
-    z_peer = hi + 8 * (1 - 2 * b3)
 
     def near(d):
         return hi + (1 - 2 * b0) * (d % 2) + 2 * (1 - 2 * b1) * (d // 2)
 
+    def far(d):
+        return hi + 4 * (1 - 2 * b2) * (d % 2) + 8 * (1 - 2 * b3) * (d // 2)
+
     barrier = pltpu.get_barrier_semaphore()
-    for to in (near(1), near(2), near(3), y_peer, z_peer):
+    for to in (near(1), near(2), near(3), far(1), far(2), far(3)):
         pl.semaphore_signal(barrier, inc=1, device_id={"hi": to, "lo": lo}, device_id_type=MESH)
 
     @pl.loop(1, n_lo)
@@ -130,7 +130,7 @@
     wb0 = middle_form(real_form(g_ref, 0, 1))
     i, j = iotas(256, 256)
     perm[...] = jnp.where(j == regrouped(i), 1.0, 0.0).astype(BF)
-    pl.semaphore_wait(barrier, 5 + n_lo - 1)
+    pl.semaphore_wait(barrier, 6 + n_lo - 1)
 
     def near_copy(ch, d):
         a = b0 + (1 - 2 * b0) * (d % 2)
@@ -156,12 +156,9 @@
         )
 
     def far_copy(k, kind):
-        src, dst, to = (
-            (m2[k], y2[k].at[1 - b3, b2], y_peer),
-            (s2[k].at[b3, 1 - b2], y2[k].at[b3, b2], y_peer),
-            (s2[k].at[1 - b3, b2], y2[k].at[b3, b2], z_peer),
-            (s2[k].at[1 - b3, 1 - b2], m2[k], z_peer),
-        )[kind]
+        a = b2 + (1 - 2 * b2) * (kind % 2)
+        b = b3 + (1 - 2 * b3) * (kind // 2)
+        src, dst, to = s2[k].at[b, a], y2[k].at[b3, b2], far(kind)
         return pltpu.make_async_remote_copy(
             src_ref=src,
             dst_ref=dst,
@@ -288,38 +285,25 @@
                 for a in range(2):
                     s2[at][n % 2, a, g * 4 + n // 2] = done[16 * a : 16 * (a + 1)]
 
-        for kind in (3, 1, 2):
+        for kind in (3, 2, 1):
             far_copy(at, kind).start()
         y2[at][b3, b2] = s2[at][b3, b2]
 
-    def pass_on(at):
-        far_copy(at, 3).wait_recv()
-        far_copy(at, 0).start()
-
-    pass_to_lo(0)
-    pass_to_lo(1)
+    for ch in range(CH):
+        pass_to_lo(ch)
     take_from_lo(0)
     take_from_lo(1)
     top_gate()
     for n_sub in range(SUB):
         middle_and_send(0, n_sub)
-    pass_to_lo(2)
-    pass_on(0)
-    pass_on(1)
-    pass_to_lo(3)
-    pass_on(2)
-    pass_on(3)
     take_from_lo(2)
     take_from_lo(3)
     top_gate()
     for n_sub in range(SUB):
         middle_and_send(1, n_sub)
-    for n_sub in range(SUB):
-        pass_on(SUB + n_sub)
-
     for ch in range(SUB):
         for e in range(2):
-            for kind in range(3):
+            for kind in range(1, 4):
                 far_copy(e * SUB + ch, kind).wait_recv()
 
         @pl.loop(0, 2)
@@ -357,7 +341,7 @@
             lo_copy(ch, j).wait_send()
 
     for at in range(2 * SUB):
-        for kind in range(4):
+        for kind in range(1, 4):
             far_copy(at, kind).wait_send()
 
 
@@ -371,7 +355,6 @@
         [pltpu.VMEM(quarter, BF)] * 8
         + [pltpu.VMEM(by_lo, BF)] * 8
         + [pltpu.VMEM((2, 2, 8, 16, 128), BF)] * 16
-        + [pltpu.VMEM((8, 16, 128), BF)] * 8
         + [pltpu.VMEM((32 * PA, 128), F32), pltpu.VMEM((64 * PB, 128), F32)]
         + [pltpu.VMEM((128, 128), BF)] * 3
         + [pltpu.VMEM((256, 256), BF)] * 2

time: 97 us -> 83.9 us (0.86)
  Pallas kernels: 93.5 us -> 80 us
    pallas_call x1, Pallas kernels: 93.5 us -> 80 us  [on_device(): pl.pallas_call(functools.partial(kernel, n_lo), out_shape=jax.ShapeDtypeS...]
where the time goes in v3:
time: 83.9 us; the launch traced here: 83.3 us
  Pallas kernels  80 us (95%)
  local copies, waits for them, and re-layouts  3.28 us (4%)
    pallas_call x1, Pallas kernels, on_device(): pl.pallas_call(functools.partial(kernel, n_lo), out_shape=jax.ShapeDtypeS...  80 us
    reshape x1, local copies, waits for them, and re-layouts, on_device(): x = state.reshape(128, 4096)  2.3 us

profile of v3, /device:TPU:1, one launch (start us, length us, event | category | flops | bytes accessed | tf_op | source)
XLA Modules:
  0.0 83.3 jit_solution(2289025315136426588)
XLA Ops:
  0.0 0.0 copy-start.1
  0.0 0.0 copy-start
  0.0 2.3 %reshape.9.x_ref = bf16[128,4096]{1,0:T(8,128)(2,1)S(1)} reshape(bf16[2,262144]{1,0:T(2,128)(2,1)} %param.3) | data formatting | bytes 2097152 | tf_op jit(solution)/shard_map/reshape | solution.py:351
  2.3 0.0 copy-done.1
  2.3 0.0 copy-done
  2.3 80.0 %circuit.1 = bf16[4096,128]{1,0:T(8,128)(2,1)S(1)} custom-call(bf16[128,4096]{1,0:T(8,128)(2,1)S(1)} %reshape.9.x_ref, bf16[4,3,2,64,64]{4,3,2,1,0:T(8,128)(2,1)S(1)} %copy-done, s32[32]{0:T(128)S(1)} %copy-done.1), custom_call_target="tpu_custom_call" | custom-call | tf_op jit(solution)/shard_map/circuit/pallas_call | solution.py:365
  82.3 1.0 %copy.6 = bf16[2,262144]{1,0:T(2,128)(2,1)} copy(bf16[2,262144]{1,0:T(2,128)(2,1)S(1)} %bitcast.5) | data formatting | bytes 2097152
Async XLA Ops:
  0.0 2.3 %copy-start.1 = (s32[32]{0:T(128)S(1)}, s32[32]{0:T(128)}, u32[]{:S(2)}) copy-start(s32[32]{0:T(128)} %rg_ref.1) | copy-start | bytes 388
  0.0 2.3 %copy-start = (bf16[4,3,2,64,64]{4,3,2,1,0:T(8,128)(2,1)S(1)}, bf16[4,3,2,64,64]{4,3,2,1,0:T(8,128)(2,1)}, u32[]{:S(2)}) copy-start(bf16[4,3,2,64,64]{4,3,2,1,0:T(8,128)(2,1)} %g_ref.1) | copy-start | bytes 589828

commit v4 on v3

--- a/solution.py
+++ b/solution.py
@@ -10,7 +10,7 @@
 BF = jnp.bfloat16
 F32 = jnp.float32
 MESH = pl.DeviceIdType.MESH
-CH = 4
+CH = 3
 SUB = 4
 PA = 129
 PB = 33
@@ -91,14 +91,14 @@
 
 
 def kernel(n_lo, x_ref, g_ref, rg_ref, o_ref, *scratch):
-    s1 = scratch[0:4]
-    y1 = scratch[4:8]
-    z1 = scratch[8:12]
-    r1 = scratch[12:16]
-    s2 = scratch[16:24]
-    y2 = scratch[24:32]
-    fa, fb, wc1, wb1, wb2, wa, perm = scratch[32:39]
-    ysend, yrecv, lsend, lrecv, psend, precv = scratch[39:45]
+    s1 = scratch[0:3]
+    y1 = scratch[3:6]
+    z1 = scratch[6:9]
+    r1 = scratch[9:12]
+    s2 = scratch[12:20]
+    y2 = scratch[20:28]
+    fa, fb, fx, wc1, wb1, wb2, wa, perm = scratch[28:36]
+    ysend, yrecv, lsend, lrecv, psend, precv = scratch[36:42]
     hi = lax.axis_index("hi")
     lo = lax.axis_index("lo")
     b0, b1, b2, b3 = hi % 2, hi // 2 % 2, hi // 4 % 2, hi // 8 % 2
@@ -121,9 +121,17 @@
 
     c0 = after(real_form(g_ref, 1, 2), real_form(g_ref, 0, 2))
 
+    @pl.loop(0, 64, unroll=8)
+    def _(c):
+        fx[pl.ds(c * PC, 64), :] = x_ref[pl.ds(pl.multiple_of(c * 64, 64), 64), :].astype(F32)
+
+    def from_fx(r):
+        parts = [fx[pl.ds(2 * r + n, 64, stride=PC), :].astype(BF) for n in range(2)]
+        return jnp.concatenate(parts, axis=0)
+
     @pl.loop(0, 16, unroll=4)
     def _(i):
-        made = mm(c0, x_ref[:, pl.ds(pl.multiple_of(i * 256, 256), 256)])
+        made = mm(c0, jnp.concatenate([from_fx(2 * i), from_fx(2 * i + 1)], axis=1))
         fa[pl.ds(2 * i * PA, 128), :] = made[:, :128]
         fa[pl.ds(2 * i * PA + PA, 128), :] = made[:, 128:]
 
@@ -196,15 +204,13 @@
                 rows.append(jnp.concatenate([re, im], axis=1))
             moved = mm(jnp.concatenate(rows, axis=0), perm[...]).astype(BF)
             for n in range(8):
-                for e in range(2):
-                    for a in range(2):
-                        s1[e * 2 + q12][n % 2, a, g * 4 + n // 2] = moved[
-                            32 * n + 16 * a : 32 * n + 16 * a + 16, 128 * e : 128 * (e + 1)
-                        ]
+                for a in range(2):
+                    both = moved[32 * n + 16 * a : 32 * n + 16 * a + 16]
+                    s1[q12][n % 2, a, g * 4 + n // 2] = both[:, :128]
+                    s1[2][n % 2, a, q12, g * 4 + n // 2] = both[:, 128:]
 
         send_near(q12)
     send_near(2)
-    send_near(3)
 
     wc1[...] = half_form(after(real_form(g_ref, 3, 2), real_form(g_ref, 2, 2)))
     wb1[...] = quarter_form(after(real_form(g_ref, 2, 1), real_form(g_ref, 1, 1)))
@@ -220,8 +226,12 @@
         @pl.loop(0, n_lo, unroll=4)
         def _(to):
             t = rg_ref[to]
-            z1[ch][to, 0] = y1[ch][t // 16, 0, t % 16]
-            z1[ch][to, 1] = y1[ch][t // 16, 1, t % 16]
+            for a in range(2):
+                if ch < 2:
+                    z1[ch][to, a] = y1[ch][t // 16, a, t % 16]
+                else:
+                    for q12 in range(2):
+                        z1[ch][to, a, q12] = y1[ch][t // 16, a, q12, t % 16]
 
         @pl.loop(1, n_lo)
         def _(j):
@@ -229,7 +239,11 @@
 
     def spread_out(ch, ref, t):
         for a in range(2):
-            fb[pl.ds((t * 2 + ch % 2) * PB + 16 * a, 16), :] = ref[t, a].astype(F32)
+            if ch < 2:
+                fb[pl.ds((t * 2 + ch) * PB + 16 * a, 16), :] = ref[t, a].astype(F32)
+            else:
+                for q12 in range(2):
+                    fb[pl.ds((t * 2 + q12) * PB + 16 * a, 16), :] = ref[t, a, q12].astype(F32)
 
     def take_from_lo(ch):
         spread_out(ch, z1[ch], lo)
@@ -237,10 +251,7 @@
         @pl.loop(1, n_lo)
         def _(j):
             lo_copy(ch, j).wait_recv()
-
-        @pl.loop(1, n_lo)
-        def _(j):
-            spread_out(ch, r1[ch], (lo + j) % n_lo)
+            spread_out(ch, r1[ch], (lo + n_lo - j) % n_lo)
 
     def top_gate():
         left = lax.broadcasted_iota(jnp.int32, (64, 128), 1) < 64
@@ -297,7 +308,6 @@
     for n_sub in range(SUB):
         middle_and_send(0, n_sub)
     take_from_lo(2)
-    take_from_lo(3)
     top_gate()
     for n_sub in range(SUB):
         middle_and_send(1, n_sub)
@@ -348,14 +358,20 @@
 def on_device(state, gates, regroup):
     n_lo = lax.axis_size("lo")
     vmem = pl.BlockSpec(memory_space=pltpu.VMEM)
-    x = state.reshape(128, 4096)
+    x = state.reshape(2, 2048, 128).transpose(1, 0, 2).reshape(4096, 128)
     quarter = (2, 2, 16, 16, 128)
     by_lo = (n_lo, 2, 16, 128)
     scratch = (
-        [pltpu.VMEM(quarter, BF)] * 8
-        + [pltpu.VMEM(by_lo, BF)] * 8
+        [pltpu.VMEM(quarter, BF)] * 2
+        + [pltpu.VMEM((2, 2, 2, 16, 16, 128), BF)]
+        + [pltpu.VMEM(quarter, BF)] * 2
+        + [pltpu.VMEM((2, 2, 2, 16, 16, 128), BF)]
+        + [pltpu.VMEM(by_lo, BF)] * 2
+        + [pltpu.VMEM((n_lo, 2, 2, 16, 128), BF)]
+        + [pltpu.VMEM(by_lo, BF)] * 2
+        + [pltpu.VMEM((n_lo, 2, 2, 16, 128), BF)]
         + [pltpu.VMEM((2, 2, 8, 16, 128), BF)] * 16
-        + [pltpu.VMEM((32 * PA, 128), F32), pltpu.VMEM((64 * PB, 128), F32)]
+        + [pltpu.VMEM((32 * PA, 128), F32), pltpu.VMEM((64 * PB, 128), F32), pltpu.VMEM((64 * PC, 128), F32)]
         + [pltpu.VMEM((128, 128), BF)] * 3
         + [pltpu.VMEM((256, 256), BF)] * 2
         + [pltpu.SemaphoreType.DMA((CH, 4))] * 2

time: 83.9 us -> 84.9 us (1.012)
    unnamed x5 -> x7, local copies, waits for them, and re-layouts: 0.98 us -> 3.85 us
    reshape x1 -> x0, local copies, waits for them, and re-layouts: 2.3 us -> none  [on_device(): x = state.reshape(128, 4096)]
where the time goes in v4:
time: 84.9 us; the launch traced here: 83.6 us
  Pallas kernels  79.8 us (94%)
  local copies, waits for them, and re-layouts  3.85 us (5%)
    pallas_call x1, Pallas kernels, on_device(): pl.pallas_call(functools.partial(kernel, n_lo), out_shape=jax.ShapeDtypeS...  79.8 us
    unnamed x7, local copies, waits for them, and re-layouts  3.85 us

profile of v4, /device:TPU:1, one launch (start us, length us, event | category | flops | bytes accessed | tf_op | source)
XLA Modules:
  0.0 83.6 jit_solution(17454318939578312151)
XLA Ops:
  0.0 0.0 copy-start.2
  0.0 0.7 copy-done.2
  0.7 0.0 copy-start
  0.7 1.2 %copy-done = bf16[2,262144]{1,0:T(2,128)(2,1)S(1)} copy-done((bf16[2,262144]{1,0:T(2,128)(2,1)S(1)}, bf16[2,262144]{1,0:T(2,128)(2,1)}, u32[]{:S(2)}) %copy-start) | copy-done | bytes 1048600
  1.9 0.0 copy-start.1
  1.9 1.0 %copy-done.1 = bf16[4,3,2,64,64]{4,3,2,1,0:T(8,128)(2,1)S(1)} copy-done((bf16[4,3,2,64,64]{4,3,2,1,0:T(8,128)(2,1)S(1)}, bf16[4,3,2,64,64]{4,3,2,1,0:T(8,128)(2,1)}, u32[]{:S(2)}) %copy-start.1) | copy-done | bytes 196632
  2.9 79.8 %circuit.1 = bf16[4096,128]{1,0:T(8,128)(2,1)S(1)} custom-call(bf16[4096,128]{1,0:T(8,128)(2,1)S(1)} %bitcast.11, bf16[4,3,2,64,64]{4,3,2,1,0:T(8,128)(2,1)S(1)} %copy-done.1, s32[32]{0:T(128)S(1)} %copy-done.2), custom_call_target="tpu_custom_call" | custom-call | tf_op jit(solution)/shard_map/circuit/pallas_call | solution.py:381
  82.7 1.0 %copy.7 = bf16[2,262144]{1,0:T(2,128)(2,1)} copy(bf16[2,262144]{1,0:T(2,128)(2,1)S(1)} %bitcast.10) | data formatting | bytes 2097152
Async XLA Ops:
  0.0 0.7 copy-start.2
  0.7 1.2 %copy-start = (bf16[2,262144]{1,0:T(2,128)(2,1)S(1)}, bf16[2,262144]{1,0:T(2,128)(2,1)}, u32[]{:S(2)}) copy-start(bf16[2,262144]{1,0:T(2,128)(2,1)} %param.3) | copy-start | bytes 3145732
  1.9 1.0 %copy-start.1 = (bf16[4,3,2,64,64]{4,3,2,1,0:T(8,128)(2,1)S(1)}, bf16[4,3,2,64,64]{4,3,2,1,0:T(8,128)(2,1)}, u32[]{:S(2)}) copy-start(bf16[4,3,2,64,64]{4,3,2,1,0:T(8,128)(2,1)} %g_ref.1) | copy-start | bytes 589828

commit v5 on v3

--- a/solution.py
+++ b/solution.py
@@ -10,7 +10,8 @@
 BF = jnp.bfloat16
 F32 = jnp.float32
 MESH = pl.DeviceIdType.MESH
-CH = 4
+CH = 5
+PIECES = ((0, 0, 8), (0, 8, 8), (1, 0, 16), (0, 0, 16), (1, 0, 16))
 SUB = 4
 PA = 129
 PB = 33
@@ -91,14 +92,14 @@
 
 
 def kernel(n_lo, x_ref, g_ref, rg_ref, o_ref, *scratch):
-    s1 = scratch[0:4]
-    y1 = scratch[4:8]
-    z1 = scratch[8:12]
-    r1 = scratch[12:16]
-    s2 = scratch[16:24]
-    y2 = scratch[24:32]
-    fa, fb, wc1, wb1, wb2, wa, perm = scratch[32:39]
-    ysend, yrecv, lsend, lrecv, psend, precv = scratch[39:45]
+    s1 = scratch[0:5]
+    y1 = scratch[5:10]
+    z1 = scratch[10:15]
+    r1 = scratch[15:20]
+    s2 = scratch[20:28]
+    y2 = scratch[28:36]
+    fa, fb, wc1, wb1, wb2, wa, perm = scratch[36:43]
+    ysend, yrecv, lsend, lrecv, psend, precv = scratch[43:49]
     hi = lax.axis_index("hi")
     lo = lax.axis_index("lo")
     b0, b1, b2, b3 = hi % 2, hi // 2 % 2, hi // 4 % 2, hi // 8 % 2
@@ -198,13 +199,18 @@
             for n in range(8):
                 for e in range(2):
                     for a in range(2):
-                        s1[e * 2 + q12][n % 2, a, g * 4 + n // 2] = moved[
-                            32 * n + 16 * a : 32 * n + 16 * a + 16, 128 * e : 128 * (e + 1)
-                        ]
-
-        send_near(q12)
-    send_near(2)
+                        tile = moved[32 * n + 16 * a : 32 * n + 16 * a + 16, 128 * e : 128 * (e + 1)]
+                        if e == 0 and q12 == 0:
+                            s1[0][n % 2, a, g * 4 + n // 2] = tile[:8]
+                            s1[1][n % 2, a, g * 4 + n // 2] = tile[8:]
+                        else:
+                            s1[e * 2 + q12 + 1][n % 2, a, g * 4 + n // 2] = tile
+
+        if q12 == 0:
+            send_near(0)
+        send_near(q12 + 1)
     send_near(3)
+    send_near(4)
 
     wc1[...] = half_form(after(real_form(g_ref, 3, 2), real_form(g_ref, 2, 2)))
     wb1[...] = quarter_form(after(real_form(g_ref, 2, 1), real_form(g_ref, 1, 1)))
@@ -229,7 +235,8 @@
 
     def spread_out(ch, ref, t):
         for a in range(2):
-            fb[pl.ds((t * 2 + ch % 2) * PB + 16 * a, 16), :] = ref[t, a].astype(F32)
+            q12, first, rows = PIECES[ch]
+            fb[pl.ds((t * 2 + q12) * PB + 16 * a + first, rows), :] = ref[t, a].astype(F32)
 
     def take_from_lo(ch):
         spread_out(ch, z1[ch], lo)
@@ -293,11 +300,12 @@
         pass_to_lo(ch)
     take_from_lo(0)
     take_from_lo(1)
+    take_from_lo(2)
     top_gate()
     for n_sub in range(SUB):
         middle_and_send(0, n_sub)
-    take_from_lo(2)
     take_from_lo(3)
+    take_from_lo(4)
     top_gate()
     for n_sub in range(SUB):
         middle_and_send(1, n_sub)
@@ -349,11 +357,9 @@
     n_lo = lax.axis_size("lo")
     vmem = pl.BlockSpec(memory_space=pltpu.VMEM)
     x = state.reshape(128, 4096)
-    quarter = (2, 2, 16, 16, 128)
-    by_lo = (n_lo, 2, 16, 128)
     scratch = (
-        [pltpu.VMEM(quarter, BF)] * 8
-        + [pltpu.VMEM(by_lo, BF)] * 8
+        [pltpu.VMEM((2, 2, 16, rows, 128), BF) for _, _, rows in PIECES] * 2
+        + [pltpu.VMEM((n_lo, 2, rows, 128), BF) for _, _, rows in PIECES] * 2
         + [pltpu.VMEM((2, 2, 8, 16, 128), BF)] * 16
         + [pltpu.VMEM((32 * PA, 128), F32), pltpu.VMEM((64 * PB, 128), F32)]
         + [pltpu.VMEM((128, 128), BF)] * 3

time: 83.9 us -> 86.1 us (1.026)
  Pallas kernels: 80 us -> 82.6 us
    pallas_call x1, Pallas kernels: 80 us -> 82.6 us  [on_device(): pl.pallas_call(functools.partial(kernel, n_lo), out_shape=jax.ShapeDtypeS...]
where the time goes in v5:
time: 86.1 us; the launch traced here: 85.9 us
  Pallas kernels  82.6 us (96%)
  local copies, waits for them, and re-layouts  3.28 us (4%)
    pallas_call x1, Pallas kernels, on_device(): pl.pallas_call(functools.partial(kernel, n_lo), out_shape=jax.ShapeDtypeS...  82.6 us
    reshape x1, local copies, waits for them, and re-layouts, on_device(): x = state.reshape(128, 4096)  2.3 us

profile of v5, /device:TPU:1, one launch (start us, length us, event | category | flops | bytes accessed | tf_op | source)
XLA Modules:
  0.0 85.9 jit_solution(13691921791426298426)
XLA Ops:
  0.0 0.0 copy-start.1
  0.0 0.0 copy-start
  0.0 2.3 %reshape.9.x_ref = bf16[128,4096]{1,0:T(8,128)(2,1)S(1)} reshape(bf16[2,262144]{1,0:T(2,128)(2,1)} %param.3) | data formatting | bytes 2097152 | tf_op jit(solution)/shard_map/reshape | solution.py:359
  2.3 0.0 copy-done.1
  2.3 0.0 copy-done
  2.3 82.6 %circuit.1 = bf16[4096,128]{1,0:T(8,128)(2,1)S(1)} custom-call(bf16[128,4096]{1,0:T(8,128)(2,1)S(1)} %reshape.9.x_ref, bf16[4,3,2,64,64]{4,3,2,1,0:T(8,128)(2,1)S(1)} %copy-done, s32[32]{0:T(128)S(1)} %copy-done.1), custom_call_target="tpu_custom_call" | custom-call | tf_op jit(solution)/shard_map/circuit/pallas_call | solution.py:371
  84.9 1.0 %copy.6 = bf16[2,262144]{1,0:T(2,128)(2,1)} copy(bf16[2,262144]{1,0:T(2,128)(2,1)S(1)} %bitcast.5) | data formatting | bytes 2097152
Async XLA Ops:
  0.0 2.3 %copy-start.1 = (s32[32]{0:T(128)S(1)}, s32[32]{0:T(128)}, u32[]{:S(2)}) copy-start(s32[32]{0:T(128)} %rg_ref.1) | copy-start | bytes 388
  0.0 2.3 %copy-start = (bf16[4,3,2,64,64]{4,3,2,1,0:T(8,128)(2,1)S(1)}, bf16[4,3,2,64,64]{4,3,2,1,0:T(8,128)(2,1)}, u32[]{:S(2)}) copy-start(bf16[4,3,2,64,64]{4,3,2,1,0:T(8,128)(2,1)} %g_ref.1) | copy-start | bytes 589828
